TPU v7x, 512 devices: a whole 4x8x8 slice. The times are simulated.
512 devices in a mesh: bx: 16 (over x, z_hi), by: 4 (over z_lo, core), bz: 8 (over y).
Axes of the slice: x: 4, y: 8, z: 8 (z_hi: 4, z_lo: 2; z = z_hi * 2 + z_lo), core: 2. Of those that a mesh axis runs over, the one named last changes fastest.
Arguments:
- forcing: float32 [256, 256, 512], P('bx', 'bz', 'by'), may hold values from -6 to 6
- start: float32 [256, 256, 512], P('bx', 'bz', 'by'), may hold values from -2 to 2
- element_class_index: int32 [64, 64, 128], P('bx', 'bz', 'by'), may hold values from 0 to 15
- class_coef: float32 [3, 16], replicated, may hold values from 0.3 to 3
Outputs:
- solution: float32 [256, 256, 512], P('bx', 'bz', 'by')
- residual: float32 [256, 256, 512], P('bx', 'bz', 'by')
All inputs are finite; a program needn't handle non-finite values.
Results may differ from a plain program's by a relative error of at most 0.015.
Values may be sent and summed in bfloat16 or wider, within the bound.
A program may use at most 64 MiB of HBM per device.

v0:
```python
import math
import jax
import jax.numpy as jnp
from jax import lax
from jax.sharding import PartitionSpec as P

CYCLES = 2
FACE_PENALTY = 2.0
DAMPING = 0.6666666666666666


def extended(value, sides, width):
    for axis, dim in sides:
        devices, length = (lax.axis_size(axis), value.shape[dim])
        up = [(i, (i + 1) % devices) for i in range(devices - 1)]
        down = [(j, i) for i, j in up]
        last = lax.slice_in_dim(value, length - width, length, axis=dim)
        first = lax.slice_in_dim(value, 0, width, axis=dim)
        before = lax.ppermute(last, axis, up)
        after = lax.ppermute(first, axis, down)
        value = jnp.concatenate([before, value, after], axis=dim)
    return value


def face_factor(count):
    edges = jnp.arange(count + 1, dtype=jnp.int32)
    return jnp.where(edges % 4 == 0, FACE_PENALTY, 1.0).astype(jnp.float32)


def edge_weights(kappa_pad):
    inner_x = kappa_pad[:, 1:-1, 1:-1]
    weight_x = face_factor(inner_x.shape[0] - 2)[:, None, None] * (
        (inner_x[:-1] + inner_x[1:]) * 0.5
    )
    inner_z = kappa_pad[1:-1, :, 1:-1]
    weight_z = face_factor(inner_z.shape[1] - 2)[None, :, None] * (
        (inner_z[:, :-1] + inner_z[:, 1:]) * 0.5
    )
    inner_y = kappa_pad[1:-1, 1:-1, :]
    quadrature_weight_y = face_factor(inner_y.shape[2] - 2)[None, None, :] * (
        (inner_y[:, :, :-1] + inner_y[:, :, 1:]) * 0.5
    )
    return (weight_x, weight_z, quadrature_weight_y)


def operator_diagonal(weights, sigma_node):
    weight_x, weight_z, quadrature_weight_y = weights
    total = sigma_node + (weight_x[:-1] + weight_x[1:])
    total = total + (weight_z[:, :-1] + weight_z[:, 1:])
    return total + (quadrature_weight_y[:, :, :-1] + quadrature_weight_y[:, :, 1:])


def apply_operator(field_pad, weights, sigma_node):
    weight_x, weight_z, quadrature_weight_y = weights
    centre = field_pad[1:-1, 1:-1, 1:-1]
    total = sigma_node * centre
    total = (
        total
        + weight_x[:-1] * (centre - field_pad[:-2, 1:-1, 1:-1])
        + weight_x[1:] * (centre - field_pad[2:, 1:-1, 1:-1])
    )
    total = (
        total
        + weight_z[:, :-1] * (centre - field_pad[1:-1, :-2, 1:-1])
        + weight_z[:, 1:] * (centre - field_pad[1:-1, 2:, 1:-1])
    )
    total = (
        total
        + quadrature_weight_y[:, :, :-1] * (centre - field_pad[1:-1, 1:-1, :-2])
        + quadrature_weight_y[:, :, 1:] * (centre - field_pad[1:-1, 1:-1, 2:])
    )
    return total


def padded_field(field):
    return extended(field, (("bx", 0), ("bz", 1), ("by", 2)), 1)


def node_field(element_values):
    return jnp.repeat(jnp.repeat(jnp.repeat(element_values, 4, 0), 4, 1), 4, 2)


def restrict_matrix():
    return (
        jnp.array(
            [[1.0, 2.0 / 3.0, 1.0 / 3.0, 0.0], [0.0, 1.0 / 3.0, 2.0 / 3.0, 1.0]], dtype=jnp.float32
        )
        * 0.5
    )


def prolong_matrix():
    return jnp.array(
        [[1.0, 0.0], [2.0 / 3.0, 1.0 / 3.0], [1.0 / 3.0, 2.0 / 3.0], [0.0, 1.0]], dtype=jnp.float32
    )


def restrict_field(field):
    count_x, count_z, count_y = (field.shape[0] // 4, field.shape[1] // 4, field.shape[2] // 4)
    blocks = field.reshape(count_x, 4, count_z, 4, count_y, 4)
    matrix = restrict_matrix()
    blocks = jnp.einsum("ai,pizjyk->pazjyk", matrix, blocks, precision=lax.Precision.HIGHEST)
    blocks = jnp.einsum("bj,pazjyk->pazbyk", matrix, blocks, precision=lax.Precision.HIGHEST)
    blocks = jnp.einsum("ck,pazbyk->pazbyc", matrix, blocks, precision=lax.Precision.HIGHEST)
    return blocks.reshape(2 * count_x, 2 * count_z, 2 * count_y)


def prolong_field(coarse):
    count_x, count_z, count_y = (coarse.shape[0] // 2, coarse.shape[1] // 2, coarse.shape[2] // 2)
    blocks = coarse.astype(jnp.float32).reshape(count_x, 2, count_z, 2, count_y, 2)
    matrix = prolong_matrix()
    blocks = jnp.einsum("ia,pazbyc->pizbyc", matrix, blocks, precision=lax.Precision.HIGHEST)
    blocks = jnp.einsum("jb,pizbyc->pizjyc", matrix, blocks, precision=lax.Precision.HIGHEST)
    blocks = jnp.einsum("kc,pizjyc->pizjyk", matrix, blocks, precision=lax.Precision.HIGHEST)
    return blocks.reshape(4 * count_x, 4 * count_z, 4 * count_y)


def sine_rows(index_zero, count):
    index_one = index_zero + 1
    product = (index_one[:, None] * index_one[None, :]).astype(jnp.float32)
    return (jnp.sin(product * (math.pi / (count + 1))) * math.sqrt(2.0 / (count + 1))).astype(
        jnp.bfloat16
    )


def spectrum_values(index_zero, count):
    return 2.0 - 2.0 * jnp.cos((index_zero + 1).astype(jnp.float32) * (math.pi / (count + 1)))


def class_values(element_class_index, class_coef):
    labels = jnp.arange(class_coef.shape[1], dtype=jnp.int32)
    onehot = (element_class_index[..., None] == labels).astype(jnp.float32)
    return tuple((jnp.sum(onehot * class_coef[row], axis=-1) for row in range(3)))


def coarse_correction(resid, kappa_mean, sigma_mean):
    count_bx, count_by, count_bz = (lax.axis_size("bx"), lax.axis_size("by"), lax.axis_size("bz"))
    coarse = restrict_field(resid).astype(jnp.bfloat16)
    pencil = lax.all_to_all(coarse, "by", split_axis=0, concat_axis=2, tiled=True)
    count_y = pencil.shape[2]
    table_y = sine_rows(jnp.arange(count_y, dtype=jnp.int32), count_y)
    pencil = jnp.dot(pencil, table_y, preferred_element_type=jnp.float32).astype(jnp.bfloat16)
    pencil = lax.all_to_all(pencil, "bz", split_axis=2, concat_axis=1, tiled=True)
    count_z = pencil.shape[1]
    table_z = sine_rows(jnp.arange(count_z, dtype=jnp.int32), count_z)
    pencil = jnp.einsum("ab,xbc->xac", table_z, pencil, preferred_element_type=jnp.float32).astype(
        jnp.bfloat16
    )
    pencil = lax.all_to_all(pencil, ("bx", "by"), split_axis=1, concat_axis=0, tiled=True)
    count_x = pencil.shape[0]
    x_index = jnp.arange(count_x, dtype=jnp.int32)
    table_x = sine_rows(x_index, count_x)
    local_z = pencil.shape[1]
    local_y = pencil.shape[2]
    z_index = (lax.axis_index("bx") * count_by + lax.axis_index("by")) * local_z + jnp.arange(
        local_z, dtype=jnp.int32
    )
    y_index = lax.axis_index("bz") * local_y + jnp.arange(local_y, dtype=jnp.int32)
    eigen_x = spectrum_values(x_index, count_x)
    eigen_z = spectrum_values(z_index, local_z * count_bx * count_by)
    eigen_y = spectrum_values(y_index, local_y * count_bz)
    eigen_sum = (
        kappa_mean * (eigen_x[:, None, None] + eigen_z[None, :, None] + eigen_y[None, None, :])
        + sigma_mean
    )
    pencil = (
        jnp.einsum("ab,bzy->azy", table_x, pencil, preferred_element_type=jnp.float32) / eigen_sum
    ).astype(jnp.bfloat16)
    pencil = jnp.einsum("ab,bzy->azy", table_x, pencil, preferred_element_type=jnp.float32).astype(
        jnp.bfloat16
    )
    pencil = lax.all_to_all(pencil, ("bx", "by"), split_axis=0, concat_axis=1, tiled=True)
    pencil = jnp.einsum("ab,xbc->xac", table_z, pencil, preferred_element_type=jnp.float32).astype(
        jnp.bfloat16
    )
    pencil = lax.all_to_all(pencil, "bz", split_axis=1, concat_axis=2, tiled=True)
    pencil = jnp.dot(pencil, table_y, preferred_element_type=jnp.float32).astype(jnp.bfloat16)
    coarse = lax.all_to_all(pencil, "by", split_axis=2, concat_axis=0, tiled=True)
    return prolong_field(coarse)


def body(forcing, start, element_class_index, class_coef):
    kappa_elem, sigma_elem, beta_elem = class_values(element_class_index, class_coef)
    kappa_node = node_field(kappa_elem)
    sigma_node = node_field(sigma_elem)
    beta_node = node_field(beta_elem)
    kappa_pad = extended(kappa_node, (("bx", 0), ("bz", 1), ("by", 2)), 1)
    weights = edge_weights(kappa_pad)
    diagonal = operator_diagonal(weights, sigma_node)
    kappa_mean = jnp.mean(class_coef[0])
    sigma_mean = jnp.mean(class_coef[1])

    def nonlinear_residual(solution):
        return (
            forcing
            - apply_operator(padded_field(solution), weights, sigma_node)
            - beta_node * solution * solution * solution
        )

    solution = start
    for iteration in range(CYCLES):
        resid = nonlinear_residual(solution)
        smooth_one = DAMPING * resid / diagonal
        smooth_two = (
            smooth_one
            + DAMPING
            * (resid - apply_operator(padded_field(smooth_one), weights, sigma_node))
            / diagonal
        )
        solution = solution + smooth_two + coarse_correction(resid, kappa_mean, sigma_mean)
    return (solution, nonlinear_residual(solution))


def solution(mesh):
    in_specs = (P("bx", "bz", "by"), P("bx", "bz", "by"), P("bx", "bz", "by"), P())
    out_specs = (P("bx", "bz", "by"), P("bx", "bz", "by"))
    return jax.shard_map(body, mesh=mesh, in_specs=in_specs, out_specs=out_specs, check_vma=False)
```

profile of v0, /device:TPU:11, one launch (start us, length us, event | category | flops | bytes accessed | tf_op | source)
XLA Modules:
  0.0 407.7 jit_solution(6416141053726972275)
XLA Ops:
  3.3 10.6 %collective-permute-start.1 = (f32[1,32,128]{2,1,0:T(8,128)S(1)}, f32[1,32,128]{2,1,0:T(8,128)S(1)}, u32[]{:S(2)}, u32[]{:S(2)}) collective-permute-start(f32[1,32,128]{2,1,0:T(8,128)S(1)} %copy.418), channel_id=1, source_target_pairs={{32,0},{64,32},{96,64},{128,96},{160,128},{192,160},{224,192},{256... | collective-permute-start | bytes 49160 | tf_op jit(solution)/shard_map/ppermute | solution.py:20
  19.0 6.1 %collective-permute-start.3 = (f32[1,32,128]{2,1,0:T(8,128)S(1)}, f32[1,32,128]{2,1,0:T(8,128)S(1)}, u32[]{:S(2)}, u32[]{:S(2)}) collective-permute-start(f32[1,32,128]{2,1,0:T(8,128)S(1)} %get-tuple-element.52), channel_id=1, source_target_pairs={{32,0},{64,32},{96,64},{128,96},{160,128},{192,160},{224,192},{256... | collective-permute-start | bytes 49160 | tf_op jit(solution)/shard_map/ppermute | solution.py:20
  39.8 4.5 %collective-permute-start.9 = (f32[18,34,1]{2,1,0:T(8,128)S(1)}, f32[18,34,1]{2,1,0:T(8,128)S(1)}, u32[]{:S(2)}, u32[]{:S(2)}) collective-permute-start(f32[18,34,1]{2,1,0:T(8,128)S(1)} %get-tuple-element.31), channel_id=1, source_target_pairs={{8,0},{16,8},{24,16},{9,1},{17,9},{25,17},{10,2},{18,10},{26,18},{... | collective-permute-start | bytes 7352 | tf_op jit(solution)/shard_map/ppermute | solution.py:20
  58.8 10.1 %reshape.196 = f32[4,4,8,4,32,4]{5,4,3,2,1,0:T(8,128)} reshape(f32[16,32,128]{2,1,0:T(8,128)S(1)} %get-tuple-element.19) | data formatting | bytes 524288 | tf_op jit(solution)/shard_map/reshape | solution.py:100
  68.9 5.9 %copy.426 = f32[4,4,8,4,32,4]{4,1,5,3,2,0:T(4,128)S(1)} copy(f32[4,4,8,4,32,4]{5,4,3,2,1,0:T(8,128)} %reshape.196) | data formatting | bytes 524288 | tf_op jit(solution)/shard_map/reshape | solution.py:100
  82.5 4.1 %all-to-all-start = ((bf16[4,2,1024]{2,1,0:T(2,128)(2,1)}), bf16[4,2,1024]{2,1,0:T(2,128)(2,1)S(1)}, u32[]{:S(2)}, u32[]{:S(2)}) async-start(bf16[4,2,1024]{2,1,0:T(2,128)(2,1)} %reshape.214), calls=%async_computation | async-start | bytes 32768 | tf_op jit(solution)/shard_map/all_to_all | solution.py:139
  92.7 7.2 %all-to-all-start.1 = ((bf16[8,2,512]{2,1,0:T(2,128)(2,1)}), bf16[8,2,512]{2,1,0:T(2,128)(2,1)S(1)}, u32[]{:S(2)}, u32[]{:S(2)}) async-start(bf16[8,2,512]{2,1,0:T(2,128)(2,1)} %reshape.216), calls=%async_computation.1 | async-start | bytes 32768 | tf_op jit(solution)/shard_map/all_to_all | solution.py:143
  101.3 4.1 %all-to-all-done.1 = bf16[8,2,512]{2,1,0:T(2,128)(2,1)S(1)} async-done(((bf16[8,2,512]{2,1,0:T(2,128)(2,1)}), bf16[8,2,512]{2,1,0:T(2,128)(2,1)S(1)}, u32[]{:S(2)}, u32[]{:S(2)}) %all-to-all-start.1) | async-done | bytes 16416 | tf_op jit(solution)/shard_map/all_to_all | solution.py:143
  106.8 9.5 %all-to-all-start.2 = ((bf16[2,128,32]{2,0,1:T(2,128)(2,1)}), bf16[2,128,32]{2,0,1:T(2,128)(2,1)S(1)}, u32[]{:S(2)}, u32[]{:S(2)}) async-start(bf16[2,128,32]{2,0,1:T(2,128)(2,1)} %copy.434), calls=%async_computation.2 | async-start | bytes 131072 | tf_op jit(solution)/shard_map/all_to_all | solution.py:149
  116.4 5.2 %collective-permute-start.13 = (f32[1,32,128]{2,1,0:T(8,128)S(1)}, f32[1,32,128]{2,1,0:T(8,128)S(1)}, u32[]{:S(2)}, u32[]{:S(2)}) collective-permute-start(f32[1,32,128]{2,1,0:T(8,128)S(1)} %get-tuple-element.51), channel_id=1, source_target_pairs={{32,0},{64,32},{96,64},{128,96},{160,128},{192,160},{224,192},{256... | collective-permute-start | bytes 49160 | tf_op jit(solution)/shard_map/ppermute | solution.py:20
  127.7 9.0 %all-to-all-start.3 = ((bf16[128,2,32]{2,1,0:T(2,128)(2,1)}), bf16[128,2,32]{2,1,0:T(2,128)(2,1)S(1)}, u32[]{:S(2)}, u32[]{:S(2)}) async-start(bf16[128,2,32]{2,1,0:T(2,128)(2,1)} %copy.438), calls=%async_computation.3 | async-start | bytes 131072 | tf_op jit(solution)/shard_map/all_to_all | solution.py:172
  147.0 4.4 %all-to-all-start.4 = ((bf16[8,2,512]{2,1,0:T(2,128)(2,1)}), bf16[8,2,512]{2,1,0:T(2,128)(2,1)S(1)}, u32[]{:S(2)}, u32[]{:S(2)}) async-start(bf16[8,2,512]{2,1,0:T(2,128)(2,1)} %reshape.218), calls=%async_computation.4 | async-start | bytes 32768 | tf_op jit(solution)/shard_map/all_to_all | solution.py:176
  151.4 5.6 %all-to-all-done.4 = bf16[8,2,512]{2,1,0:T(2,128)(2,1)S(1)} async-done(((bf16[8,2,512]{2,1,0:T(2,128)(2,1)}), bf16[8,2,512]{2,1,0:T(2,128)(2,1)S(1)}, u32[]{:S(2)}, u32[]{:S(2)}) %all-to-all-start.4) | async-done | bytes 16416 | tf_op jit(solution)/shard_map/all_to_all | solution.py:176
  160.0 4.6 %all-to-all-start.5 = ((bf16[4,2,1024]{2,1,0:T(2,128)(2,1)}), bf16[4,2,1024]{2,1,0:T(2,128)(2,1)S(1)}, u32[]{:S(2)}, u32[]{:S(2)}) async-start(bf16[4,2,1024]{2,1,0:T(2,128)(2,1)} %reshape.220), calls=%async_computation.5 | async-start | bytes 32768 | tf_op jit(solution)/shard_map/all_to_all | solution.py:178
  174.7 15.5 %fusion.9 = f32[4,4,8,4,32,4]{5,4,3,2,1,0:T(8,128)} fusion(f32[4,2,1,1,1,1]{0,1,5,4,3,2:T(2,128)S(1)} %copy-done.13, f32[4,4,8,4,32,2]{4,3,5,2,1,0:T(4,128)S(1)} %convolution_bitcast_fusion.2), kind=kOutput, calls=%fused_computation.37 | convolution fusion | flops 1572864 | bytes 393248 | tf_op jit(solution)/shard_map/kc,pizjyc->pizjyk/dot_general | solution.py:114
  190.2 8.2 %reshape.198 = f32[16,32,128]{2,1,0:T(8,128)S(1)} reshape(f32[4,4,8,4,32,4]{5,4,3,2,1,0:T(8,128)} %fusion.9) | data formatting | bytes 524288 | tf_op jit(solution)/shard_map/reshape | solution.py:115
  206.2 4.6 %collective-permute-done.18 = f32[1,32,128]{2,1,0:T(8,128)S(1)} collective-permute-done((f32[1,32,128]{2,1,0:T(8,128)S(1)}, f32[1,32,128]{2,1,0:T(8,128)S(1)}, u32[]{:S(2)}, u32[]{:S(2)}) %collective-permute-start.18) | collective-permute-done | bytes 16416 | tf_op jit(solution)/shard_map/ppermute | solution.py:19
  218.5 4.3 %collective-permute-start.23 = (f32[18,34,1]{2,1,0:T(8,128)S(1)}, f32[18,34,1]{2,1,0:T(8,128)S(1)}, u32[]{:S(2)}, u32[]{:S(2)}) collective-permute-start(f32[18,34,1]{2,1,0:T(8,128)S(1)} %get-tuple-element.25), channel_id=1, source_target_pairs={{8,0},{16,8},{24,16},{9,1},{17,9},{25,17},{10,2},{18,10},{26,18},{... | collective-permute-start | bytes 7352 | tf_op jit(solution)/shard_map/ppermute | solution.py:20
  232.9 10.1 %reshape.199 = f32[4,4,8,4,32,4]{5,4,3,2,1,0:T(8,128)} reshape(f32[16,32,128]{2,1,0:T(8,128)S(1)} %get-tuple-element.16) | data formatting | bytes 524288 | tf_op jit(solution)/shard_map/reshape | solution.py:100
  243.0 5.9 %copy.454 = f32[4,4,8,4,32,4]{4,1,5,3,2,0:T(4,128)S(1)} copy(f32[4,4,8,4,32,4]{5,4,3,2,1,0:T(8,128)} %reshape.199) | data formatting | bytes 524288 | tf_op jit(solution)/shard_map/reshape | solution.py:100
  256.8 7.1 %all_to_all.210 = bf16[4,2,1024]{2,1,0:T(2,128)(2,1)S(1)} all-to-all(bf16[4,2,1024]{2,1,0:T(2,128)(2,1)S(1)} %reshape.222), channel_id=1, replica_groups=mesh['bx'=16,'by'=4,'bz'=8] {'by'}, dimensions={0} | all-to-all | bytes 32768 | tf_op jit(solution)/shard_map/all_to_all | solution.py:139
  266.2 10.5 %all_to_all.211 = bf16[8,2,512]{2,1,0:T(2,128)(2,1)S(1)} all-to-all(bf16[8,2,512]{2,1,0:T(2,128)(2,1)S(1)} %reshape.224), channel_id=1, replica_groups=mesh['bx'=16,'by'=4,'bz'=8] {'bz'}, dimensions={0} | all-to-all | bytes 32768 | tf_op jit(solution)/shard_map/all_to_all | solution.py:143
  278.9 7.7 %all-to-all-start.8 = ((bf16[2,128,32]{2,0,1:T(2,128)(2,1)}), bf16[2,128,32]{2,0,1:T(2,128)(2,1)S(1)}, u32[]{:S(2)}, u32[]{:S(2)}) async-start(bf16[2,128,32]{2,0,1:T(2,128)(2,1)} %copy.462), calls=%async_computation.8 | async-start | bytes 131072 | tf_op jit(solution)/shard_map/all_to_all | solution.py:149
  286.6 5.2 %collective-permute-start.25 = (f32[1,32,128]{2,1,0:T(8,128)S(1)}, f32[1,32,128]{2,1,0:T(8,128)S(1)}, u32[]{:S(2)}, u32[]{:S(2)}) collective-permute-start(f32[1,32,128]{2,1,0:T(8,128)S(1)} %get-tuple-element.47), channel_id=1, source_target_pairs={{32,0},{64,32},{96,64},{128,96},{160,128},{192,160},{224,192},{256... | collective-permute-start | bytes 49160 | tf_op jit(solution)/shard_map/ppermute | solution.py:20
  299.3 8.6 %all-to-all-start.9 = ((bf16[128,2,32]{2,1,0:T(2,128)(2,1)}), bf16[128,2,32]{2,1,0:T(2,128)(2,1)S(1)}, u32[]{:S(2)}, u32[]{:S(2)}) async-start(bf16[128,2,32]{2,1,0:T(2,128)(2,1)} %copy.466), calls=%async_computation.9 | async-start | bytes 131072 | tf_op jit(solution)/shard_map/all_to_all | solution.py:172
  318.8 4.4 %all-to-all-start.10 = ((bf16[8,2,512]{2,1,0:T(2,128)(2,1)}), bf16[8,2,512]{2,1,0:T(2,128)(2,1)S(1)}, u32[]{:S(2)}, u32[]{:S(2)}) async-start(bf16[8,2,512]{2,1,0:T(2,128)(2,1)} %reshape.226), calls=%async_computation.10 | async-start | bytes 32768 | tf_op jit(solution)/shard_map/all_to_all | solution.py:176
  323.8 5.0 %all-to-all-done.10 = bf16[8,2,512]{2,1,0:T(2,128)(2,1)S(1)} async-done(((bf16[8,2,512]{2,1,0:T(2,128)(2,1)}), bf16[8,2,512]{2,1,0:T(2,128)(2,1)S(1)}, u32[]{:S(2)}, u32[]{:S(2)}) %all-to-all-start.10) | async-done | bytes 16416 | tf_op jit(solution)/shard_map/all_to_all | solution.py:176
  331.8 4.6 %all-to-all-start.11 = ((bf16[4,2,1024]{2,1,0:T(2,128)(2,1)}), bf16[4,2,1024]{2,1,0:T(2,128)(2,1)S(1)}, u32[]{:S(2)}, u32[]{:S(2)}) async-start(bf16[4,2,1024]{2,1,0:T(2,128)(2,1)} %reshape.228), calls=%async_computation.11 | async-start | bytes 32768 | tf_op jit(solution)/shard_map/all_to_all | solution.py:178
  348.0 16.2 %fusion.6 = f32[4,4,8,4,32,4]{5,4,3,2,1,0:T(8,128)} fusion(f32[4,2,1,1,1,1]{0,1,5,4,3,2:T(2,128)} %constant.103, f32[4,4,8,4,32,2]{4,3,5,2,1,0:T(4,128)S(1)} %convolution_bitcast_fusion), kind=kOutput, calls=%fused_computation.34 | convolution fusion | flops 1572864 | bytes 393248 | tf_op jit(solution)/shard_map/kc,pizjyc->pizjyk/dot_general | solution.py:114
  364.3 8.8 %reshape.201 = f32[16,32,128]{2,1,0:T(8,128)} reshape(f32[4,4,8,4,32,4]{5,4,3,2,1,0:T(8,128)} %fusion.6) | data formatting | bytes 524288 | tf_op jit(solution)/shard_map/reshape | solution.py:115
  381.7 4.6 %collective-permute-done.30 = f32[1,32,128]{2,1,0:T(8,128)S(1)} collective-permute-done((f32[1,32,128]{2,1,0:T(8,128)S(1)}, f32[1,32,128]{2,1,0:T(8,128)S(1)}, u32[]{:S(2)}, u32[]{:S(2)}) %collective-permute-start.30) | collective-permute-done | bytes 16416 | tf_op jit(solution)/shard_map/ppermute | solution.py:19
  394.1 4.3 %collective-permute-start.35 = (f32[18,34,1]{2,1,0:T(8,128)S(1)}, f32[18,34,1]{2,1,0:T(8,128)S(1)}, u32[]{:S(2)}, u32[]{:S(2)}) collective-permute-start(f32[18,34,1]{2,1,0:T(8,128)S(1)} %get-tuple-element.21), channel_id=1, source_target_pairs={{8,0},{16,8},{24,16},{9,1},{17,9},{25,17},{10,2},{18,10},{26,18},{... | collective-permute-start | bytes 7352 | tf_op jit(solution)/shard_map/ppermute | solution.py:20
  (264 shorter events, 177.5 us)
Async XLA Ops:
  3.3 25.4 %collective-permute-start.1 = (f32[1,32,128]{2,1,0:T(8,128)S(1)}, f32[1,32,128]{2,1,0:T(8,128)S(1)}, u32[]{:S(2)}, u32[]{:S(2)}) collective-permute-start(f32[1,32,128]{2,1,0:T(8,128)S(1)} %copy.418), channel_id=1, source_target_pairs={{32,0},{64,32},{96,64},{128,96},{160,128},{192,160},{224,192},{256... | collective-permute-start | bytes 49160 | tf_op jit(solution)/shard_map/ppermute | solution.py:20
  14.1 14.6 %collective-permute-start = (f32[1,32,128]{2,1,0:T(8,128)S(1)}, f32[1,32,128]{2,1,0:T(8,128)S(1)}, u32[]{:S(2)}, u32[]{:S(2)}) collective-permute-start(f32[1,32,128]{2,1,0:T(8,128)S(1)} %copy.414), channel_id=1, source_target_pairs={{0,32},{32,64},{64,96},{96,128},{128,160},{160,192},{192,224},{224... | collective-permute-start | bytes 49160 | tf_op jit(solution)/shard_map/ppermute | solution.py:19
  16.8 17.2 %collective-permute-start.2 = (f32[1,32,128]{2,1,0:T(8,128)S(1)}, f32[1,32,128]{2,1,0:T(8,128)S(1)}, u32[]{:S(2)}, u32[]{:S(2)}) collective-permute-start(f32[1,32,128]{2,1,0:T(8,128)S(1)} %get-tuple-element.53), channel_id=1, source_target_pairs={{0,32},{32,64},{64,96},{96,128},{128,160},{160,192},{192,224},{224... | collective-permute-start | bytes 49160 | tf_op jit(solution)/shard_map/ppermute | solution.py:19
  19.0 15.1 %collective-permute-start.3 = (f32[1,32,128]{2,1,0:T(8,128)S(1)}, f32[1,32,128]{2,1,0:T(8,128)S(1)}, u32[]{:S(2)}, u32[]{:S(2)}) collective-permute-start(f32[1,32,128]{2,1,0:T(8,128)S(1)} %get-tuple-element.52), channel_id=1, source_target_pairs={{32,0},{64,32},{96,64},{128,96},{160,128},{192,160},{224,192},{256... | collective-permute-start | bytes 49160 | tf_op jit(solution)/shard_map/ppermute | solution.py:20
  28.7 10.8 %collective-permute-start.5 = (f32[18,1,128]{2,1,0:T(1,128)S(1)}, f32[18,1,128]{2,1,0:T(1,128)S(1)}, u32[]{:S(2)}, u32[]{:S(2)}) collective-permute-start(f32[18,1,128]{2,1,0:T(1,128)S(1)} %get-tuple-element.43), channel_id=1, source_target_pairs={{1,0},{2,1},{3,2},{4,3},{5,4},{6,5},{7,6},{9,8},{10,9},{11,10},{12... | collective-permute-start | bytes 27656 | tf_op jit(solution)/shard_map/ppermute | solution.py:20
  34.1 13.2 %collective-permute-start.7 = (f32[18,1,128]{2,1,0:T(1,128)S(1)}, f32[18,1,128]{2,1,0:T(1,128)S(1)}, u32[]{:S(2)}, u32[]{:S(2)}) collective-permute-start(f32[18,1,128]{2,1,0:T(1,128)S(1)} %get-tuple-element.41), channel_id=1, source_target_pairs={{1,0},{2,1},{3,2},{4,3},{5,4},{6,5},{7,6},{9,8},{10,9},{11,10},{12... | collective-permute-start | bytes 27656 | tf_op jit(solution)/shard_map/ppermute | solution.py:20
  36.2 11.1 %collective-permute-start.6 = (f32[18,1,128]{2,1,0:T(1,128)S(1)}, f32[18,1,128]{2,1,0:T(1,128)S(1)}, u32[]{:S(2)}, u32[]{:S(2)}) collective-permute-start(f32[18,1,128]{2,1,0:T(1,128)S(1)} %get-tuple-element.40), channel_id=1, source_target_pairs={{0,1},{1,2},{2,3},{3,4},{4,5},{5,6},{6,7},{8,9},{9,10},{10,11},{11... | collective-permute-start | bytes 27656 | tf_op jit(solution)/shard_map/ppermute | solution.py:19
  39.8 13.7 %collective-permute-start.9 = (f32[18,34,1]{2,1,0:T(8,128)S(1)}, f32[18,34,1]{2,1,0:T(8,128)S(1)}, u32[]{:S(2)}, u32[]{:S(2)}) collective-permute-start(f32[18,34,1]{2,1,0:T(8,128)S(1)} %get-tuple-element.31), channel_id=1, source_target_pairs={{8,0},{16,8},{24,16},{9,1},{17,9},{25,17},{10,2},{18,10},{26,18},{... | collective-permute-start | bytes 7352 | tf_op jit(solution)/shard_map/ppermute | solution.py:20
  44.3 9.1 %collective-permute-start.8 = (f32[18,34,1]{2,1,0:T(8,128)S(1)}, f32[18,34,1]{2,1,0:T(8,128)S(1)}, u32[]{:S(2)}, u32[]{:S(2)}) collective-permute-start(f32[18,34,1]{2,1,0:T(8,128)S(1)} %get-tuple-element.30), channel_id=1, source_target_pairs={{0,8},{8,16},{16,24},{1,9},{9,17},{17,25},{2,10},{10,18},{18,26},{... | collective-permute-start | bytes 7352 | tf_op jit(solution)/shard_map/ppermute | solution.py:19
  92.7 12.7 %all-to-all-start.1 = ((bf16[8,2,512]{2,1,0:T(2,128)(2,1)}), bf16[8,2,512]{2,1,0:T(2,128)(2,1)S(1)}, u32[]{:S(2)}, u32[]{:S(2)}) async-start(bf16[8,2,512]{2,1,0:T(2,128)(2,1)} %reshape.216), calls=%async_computation.1 | async-start | bytes 32768 | tf_op jit(solution)/shard_map/all_to_all | solution.py:143
  106.8 18.4 %all-to-all-start.2 = ((bf16[2,128,32]{2,0,1:T(2,128)(2,1)}), bf16[2,128,32]{2,0,1:T(2,128)(2,1)S(1)}, u32[]{:S(2)}, u32[]{:S(2)}) async-start(bf16[2,128,32]{2,0,1:T(2,128)(2,1)} %copy.434), calls=%async_computation.2 | async-start | bytes 131072 | tf_op jit(solution)/shard_map/all_to_all | solution.py:149
  116.4 20.4 %collective-permute-start.13 = (f32[1,32,128]{2,1,0:T(8,128)S(1)}, f32[1,32,128]{2,1,0:T(8,128)S(1)}, u32[]{:S(2)}, u32[]{:S(2)}) collective-permute-start(f32[1,32,128]{2,1,0:T(8,128)S(1)} %get-tuple-element.51), channel_id=1, source_target_pairs={{32,0},{64,32},{96,64},{128,96},{160,128},{192,160},{224,192},{256... | collective-permute-start | bytes 49160 | tf_op jit(solution)/shard_map/ppermute | solution.py:20
  121.6 15.2 %collective-permute-start.12 = (f32[1,32,128]{2,1,0:T(8,128)S(1)}, f32[1,32,128]{2,1,0:T(8,128)S(1)}, u32[]{:S(2)}, u32[]{:S(2)}) collective-permute-start(f32[1,32,128]{2,1,0:T(8,128)S(1)} %get-tuple-element.50), channel_id=1, source_target_pairs={{0,32},{32,64},{64,96},{96,128},{128,160},{160,192},{192,224},{224... | collective-permute-start | bytes 49160 | tf_op jit(solution)/shard_map/ppermute | solution.py:19
  127.7 17.9 %all-to-all-start.3 = ((bf16[128,2,32]{2,1,0:T(2,128)(2,1)}), bf16[128,2,32]{2,1,0:T(2,128)(2,1)S(1)}, u32[]{:S(2)}, u32[]{:S(2)}) async-start(bf16[128,2,32]{2,1,0:T(2,128)(2,1)} %copy.438), calls=%async_computation.3 | async-start | bytes 131072 | tf_op jit(solution)/shard_map/all_to_all | solution.py:172
  136.8 14.5 %collective-permute-start.15 = (f32[18,1,128]{2,1,0:T(1,128)S(1)}, f32[18,1,128]{2,1,0:T(1,128)S(1)}, u32[]{:S(2)}, u32[]{:S(2)}) collective-permute-start(f32[18,1,128]{2,1,0:T(1,128)S(1)} %get-tuple-element.39), channel_id=1, source_target_pairs={{1,0},{2,1},{3,2},{4,3},{5,4},{6,5},{7,6},{9,8},{10,9},{11,10},{12... | collective-permute-start | bytes 27656 | tf_op jit(solution)/shard_map/ppermute | solution.py:20
  139.9 11.5 %collective-permute-start.14 = (f32[18,1,128]{2,1,0:T(1,128)S(1)}, f32[18,1,128]{2,1,0:T(1,128)S(1)}, u32[]{:S(2)}, u32[]{:S(2)}) collective-permute-start(f32[18,1,128]{2,1,0:T(1,128)S(1)} %get-tuple-element.38), channel_id=1, source_target_pairs={{0,1},{1,2},{2,3},{3,4},{4,5},{5,6},{6,7},{8,9},{9,10},{10,11},{11... | collective-permute-start | bytes 27656 | tf_op jit(solution)/shard_map/ppermute | solution.py:19
  147.0 10.0 %all-to-all-start.4 = ((bf16[8,2,512]{2,1,0:T(2,128)(2,1)}), bf16[8,2,512]{2,1,0:T(2,128)(2,1)S(1)}, u32[]{:S(2)}, u32[]{:S(2)}) async-start(bf16[8,2,512]{2,1,0:T(2,128)(2,1)} %reshape.218), calls=%async_computation.4 | async-start | bytes 32768 | tf_op jit(solution)/shard_map/all_to_all | solution.py:176
  160.0 11.2 %all-to-all-start.5 = ((bf16[4,2,1024]{2,1,0:T(2,128)(2,1)}), bf16[4,2,1024]{2,1,0:T(2,128)(2,1)S(1)}, u32[]{:S(2)}, u32[]{:S(2)}) async-start(bf16[4,2,1024]{2,1,0:T(2,128)(2,1)} %reshape.220), calls=%async_computation.5 | async-start | bytes 32768 | tf_op jit(solution)/shard_map/all_to_all | solution.py:178
  165.6 32.7 %collective-permute-start.17 = (f32[18,34,1]{2,1,0:T(8,128)}, f32[18,34,1]{2,1,0:T(8,128)}, u32[]{:S(2)}, u32[]{:S(2)}) collective-permute-start(f32[18,34,1]{2,1,0:T(8,128)} %get-tuple-element.27), channel_id=1, source_target_pairs={{8,0},{16,8},{24,16},{9,1},{17,9},{25,17},{10,2},{18,10},{26,18},{... | collective-permute-start | bytes 7352 | tf_op jit(solution)/shard_map/ppermute | solution.py:20
  167.6 30.8 %collective-permute-start.16 = (f32[18,34,1]{2,1,0:T(8,128)}, f32[18,34,1]{2,1,0:T(8,128)}, u32[]{:S(2)}, u32[]{:S(2)}) collective-permute-start(f32[18,34,1]{2,1,0:T(8,128)} %get-tuple-element.26), channel_id=1, source_target_pairs={{0,8},{8,16},{16,24},{1,9},{9,17},{17,25},{2,10},{10,18},{18,26},{... | collective-permute-start | bytes 7352 | tf_op jit(solution)/shard_map/ppermute | solution.py:19
  218.5 11.1 %collective-permute-start.23 = (f32[18,34,1]{2,1,0:T(8,128)S(1)}, f32[18,34,1]{2,1,0:T(8,128)S(1)}, u32[]{:S(2)}, u32[]{:S(2)}) collective-permute-start(f32[18,34,1]{2,1,0:T(8,128)S(1)} %get-tuple-element.25), channel_id=1, source_target_pairs={{8,0},{16,8},{24,16},{9,1},{17,9},{25,17},{10,2},{18,10},{26,18},{... | collective-permute-start | bytes 7352 | tf_op jit(solution)/shard_map/ppermute | solution.py:20
  278.9 16.5 %all-to-all-start.8 = ((bf16[2,128,32]{2,0,1:T(2,128)(2,1)}), bf16[2,128,32]{2,0,1:T(2,128)(2,1)S(1)}, u32[]{:S(2)}, u32[]{:S(2)}) async-start(bf16[2,128,32]{2,0,1:T(2,128)(2,1)} %copy.462), calls=%async_computation.8 | async-start | bytes 131072 | tf_op jit(solution)/shard_map/all_to_all | solution.py:149
  286.6 21.4 %collective-permute-start.25 = (f32[1,32,128]{2,1,0:T(8,128)S(1)}, f32[1,32,128]{2,1,0:T(8,128)S(1)}, u32[]{:S(2)}, u32[]{:S(2)}) collective-permute-start(f32[1,32,128]{2,1,0:T(8,128)S(1)} %get-tuple-element.47), channel_id=1, source_target_pairs={{32,0},{64,32},{96,64},{128,96},{160,128},{192,160},{224,192},{256... | collective-permute-start | bytes 49160 | tf_op jit(solution)/shard_map/ppermute | solution.py:20
  291.8 16.2 %collective-permute-start.24 = (f32[1,32,128]{2,1,0:T(8,128)S(1)}, f32[1,32,128]{2,1,0:T(8,128)S(1)}, u32[]{:S(2)}, u32[]{:S(2)}) collective-permute-start(f32[1,32,128]{2,1,0:T(8,128)S(1)} %get-tuple-element.46), channel_id=1, source_target_pairs={{0,32},{32,64},{64,96},{96,128},{128,160},{160,192},{192,224},{224... | collective-permute-start | bytes 49160 | tf_op jit(solution)/shard_map/ppermute | solution.py:19
  299.3 17.5 %all-to-all-start.9 = ((bf16[128,2,32]{2,1,0:T(2,128)(2,1)}), bf16[128,2,32]{2,1,0:T(2,128)(2,1)S(1)}, u32[]{:S(2)}, u32[]{:S(2)}) async-start(bf16[128,2,32]{2,1,0:T(2,128)(2,1)} %copy.466), calls=%async_computation.9 | async-start | bytes 131072 | tf_op jit(solution)/shard_map/all_to_all | solution.py:172
  308.0 15.2 %collective-permute-start.27 = (f32[18,1,128]{2,1,0:T(1,128)S(1)}, f32[18,1,128]{2,1,0:T(1,128)S(1)}, u32[]{:S(2)}, u32[]{:S(2)}) collective-permute-start(f32[18,1,128]{2,1,0:T(1,128)S(1)} %get-tuple-element.35), channel_id=1, source_target_pairs={{1,0},{2,1},{3,2},{4,3},{5,4},{6,5},{7,6},{9,8},{10,9},{11,10},{12... | collective-permute-start | bytes 27656 | tf_op jit(solution)/shard_map/ppermute | solution.py:20
  311.0 12.1 %collective-permute-start.26 = (f32[18,1,128]{2,1,0:T(1,128)S(1)}, f32[18,1,128]{2,1,0:T(1,128)S(1)}, u32[]{:S(2)}, u32[]{:S(2)}) collective-permute-start(f32[18,1,128]{2,1,0:T(1,128)S(1)} %get-tuple-element.34), channel_id=1, source_target_pairs={{0,1},{1,2},{2,3},{3,4},{4,5},{5,6},{6,7},{8,9},{9,10},{10,11},{11... | collective-permute-start | bytes 27656 | tf_op jit(solution)/shard_map/ppermute | solution.py:19
  318.8 10.0 %all-to-all-start.10 = ((bf16[8,2,512]{2,1,0:T(2,128)(2,1)}), bf16[8,2,512]{2,1,0:T(2,128)(2,1)S(1)}, u32[]{:S(2)}, u32[]{:S(2)}) async-start(bf16[8,2,512]{2,1,0:T(2,128)(2,1)} %reshape.226), calls=%async_computation.10 | async-start | bytes 32768 | tf_op jit(solution)/shard_map/all_to_all | solution.py:176
  331.8 11.4 %all-to-all-start.11 = ((bf16[4,2,1024]{2,1,0:T(2,128)(2,1)}), bf16[4,2,1024]{2,1,0:T(2,128)(2,1)S(1)}, u32[]{:S(2)}, u32[]{:S(2)}) async-start(bf16[4,2,1024]{2,1,0:T(2,128)(2,1)} %reshape.228), calls=%async_computation.11 | async-start | bytes 32768 | tf_op jit(solution)/shard_map/all_to_all | solution.py:178
  337.4 35.7 %collective-permute-start.29 = (f32[18,34,1]{2,1,0:T(8,128)}, f32[18,34,1]{2,1,0:T(8,128)}, u32[]{:S(2)}, u32[]{:S(2)}) collective-permute-start(f32[18,34,1]{2,1,0:T(8,128)} %get-tuple-element.23), channel_id=1, source_target_pairs={{8,0},{16,8},{24,16},{9,1},{17,9},{25,17},{10,2},{18,10},{26,18},{... | collective-permute-start | bytes 7352 | tf_op jit(solution)/shard_map/ppermute | solution.py:20
  339.3 33.8 %collective-permute-start.28 = (f32[18,34,1]{2,1,0:T(8,128)}, f32[18,34,1]{2,1,0:T(8,128)}, u32[]{:S(2)}, u32[]{:S(2)}) collective-permute-start(f32[18,34,1]{2,1,0:T(8,128)} %get-tuple-element.22), channel_id=1, source_target_pairs={{0,8},{8,16},{16,24},{1,9},{9,17},{17,25},{2,10},{10,18},{18,26},{... | collective-permute-start | bytes 7352 | tf_op jit(solution)/shard_map/ppermute | solution.py:19
  394.1 11.1 %collective-permute-start.35 = (f32[18,34,1]{2,1,0:T(8,128)S(1)}, f32[18,34,1]{2,1,0:T(8,128)S(1)}, u32[]{:S(2)}, u32[]{:S(2)}) collective-permute-start(f32[18,34,1]{2,1,0:T(8,128)S(1)} %get-tuple-element.21), channel_id=1, source_target_pairs={{8,0},{16,8},{24,16},{9,1},{17,9},{25,17},{10,2},{18,10},{26,18},{... | collective-permute-start | bytes 7352 | tf_op jit(solution)/shard_map/ppermute | solution.py:20
  (34 other events, 813.7 us)
where the time goes:
time: 413 us; the launch traced here: 408 us
  starting transfers between devices  184 us (45%)
  local copies, waits for them, and re-layouts  76.9 us (19%)
  matrix products  57.7 us (14%)
  waiting for transfers between devices  53.9 us (13%)
  blocking collectives  17.6 us (4%)
  other arithmetic  13.9 us (3%)
    ppermute x18, starting transfers between devices, extended(): after = lax.ppermute(first, axis, down)  69.1 us
    ppermute x18, starting transfers between devices, extended(): before = lax.ppermute(last, axis, up)  50.9 us
    reshape x4, local copies, waits for them, and re-layouts, restrict_field(): blocks = field.reshape(count_x, 4, count_z, 4, count_y, 4)  31.9 us
    dot_general x2, matrix products, prolong_field(): jnp.einsum('kc,pizjyc->pizjyk', matrix, blocks, precision=lax.Precision.H...  31.7 us
    all_to_all x2, starting transfers between devices, coarse_correction(): lax.all_to_all(pencil, ('bx', 'by'), split_axis=0, concat_axis=1, tiled=T...  17.7 us
    all_to_all x2, starting transfers between devices, coarse_correction(): lax.all_to_all(pencil, ('bx', 'by'), split_axis=1, concat_axis=0, tiled=T...  17.2 us
    reshape x2, local copies, waits for them, and re-layouts, prolong_field(): return blocks.reshape(4 * count_x, 4 * count_z, 4 * count_y)  17 us
    ppermute x18, waiting for transfers between devices, extended(): before = lax.ppermute(last, axis, up)  17 us
  transfers between devices with their start and end apart: 46, of which 18 were waited for; matrix products, arithmetic and copies ran while one was open for 18% of the time, Pallas kernels for 0%

commit v1 on v0

--- a/solution.py
+++ b/solution.py
@@ -169,7 +169,12 @@
     pencil = jnp.einsum("ab,bzy->azy", table_x, pencil, preferred_element_type=jnp.float32).astype(
         jnp.bfloat16
     )
-    pencil = lax.all_to_all(pencil, ("bx", "by"), split_axis=0, concat_axis=1, tiled=True)
+    pencil = jnp.concatenate(
+        lax.all_to_all(
+            jnp.stack(jnp.split(pencil, lax.axis_size(("bx", "by")), axis=0)), ("bx", "by"), 0, 0
+        ),
+        axis=1,
+    )
     pencil = jnp.einsum("ab,xbc->xac", table_z, pencil, preferred_element_type=jnp.float32).astype(
         jnp.bfloat16
     )

time: 413 us -> 518 us (1.25)
  local copies, waits for them, and re-layouts: 76.9 us -> 179 us
    unnamed x58 -> x184, local copies, waits for them, and re-layouts: 7.01 us -> 87.2 us
    split x0 -> x136, local copies, waits for them, and re-layouts: none -> 21.6 us  [coarse_correction(): jnp.split(pencil, lax.axis_size(('bx', 'by')), axis=0)]
  transfers between devices with their start and end apart: 46 -> 46, of which waited for: 18 -> 18; matrix products, arithmetic and copies ran while one was open for 18% -> 35% of each run, Pallas kernels for 0% -> 0%
where the time goes in v1:
time: 518 us; the launch traced here: 512 us
  starting transfers between devices  185 us (36%)
  local copies, waits for them, and re-layouts  179 us (35%)
  matrix products  58.6 us (11%)
  waiting for transfers between devices  53 us (10%)
  blocking collectives  17.6 us (3%)
  other arithmetic  13.8 us (3%)
    unnamed x184, local copies, waits for them, and re-layouts  87.2 us
    ppermute x18, starting transfers between devices, extended(): after = lax.ppermute(first, axis, down)  69 us
    ppermute x18, starting transfers between devices, extended(): before = lax.ppermute(last, axis, up)  51.2 us
    reshape x4, local copies, waits for them, and re-layouts, restrict_field(): blocks = field.reshape(count_x, 4, count_z, 4, count_y, 4)  31.9 us
    dot_general x2, matrix products, prolong_field(): jnp.einsum('kc,pizjyc->pizjyk', matrix, blocks, precision=lax.Precision.H...  31.8 us
    split x136, local copies, waits for them, and re-layouts, coarse_correction(): jnp.split(pencil, lax.axis_size(('bx', 'by')), axis=0)  21.6 us
    all_to_all x2, starting transfers between devices, coarse_correction(): lax.all_to_all(jnp.stack(jnp.split(pencil, lax.axis_size(('bx', 'by')), a...  18.7 us
    all_to_all x2, starting transfers between devices, coarse_correction(): lax.all_to_all(pencil, ('bx', 'by'), split_axis=1, concat_axis=0, tiled=T...  17.2 us
  transfers between devices with their start and end apart: 46, of which 18 were waited for; matrix products, arithmetic and copies ran while one was open for 35% of the time, Pallas kernels for 0%

profile of v1, /device:TPU:11, one launch (start us, length us, event | category | flops | bytes accessed | tf_op | source)
XLA Modules:
  0.0 511.5 jit_solution(17565877623093549326)
XLA Ops:
  3.3 10.6 %collective-permute-start.1 = (f32[1,32,128]{2,1,0:T(8,128)S(1)}, f32[1,32,128]{2,1,0:T(8,128)S(1)}, u32[]{:S(2)}, u32[]{:S(2)}) collective-permute-start(f32[1,32,128]{2,1,0:T(8,128)S(1)} %copy.1046), channel_id=1, source_target_pairs={{32,0},{64,32},{96,64},{128,96},{160,128},{192,160},{224,192},{256... | collective-permute-start | bytes 49160 | tf_op jit(solution)/shard_map/ppermute | solution.py:20
  19.0 6.1 %collective-permute-start.3 = (f32[1,32,128]{2,1,0:T(8,128)S(1)}, f32[1,32,128]{2,1,0:T(8,128)S(1)}, u32[]{:S(2)}, u32[]{:S(2)}) collective-permute-start(f32[1,32,128]{2,1,0:T(8,128)S(1)} %get-tuple-element.52), channel_id=1, source_target_pairs={{32,0},{64,32},{96,64},{128,96},{160,128},{192,160},{224,192},{256... | collective-permute-start | bytes 49160 | tf_op jit(solution)/shard_map/ppermute | solution.py:20
  39.8 4.5 collective-permute-start.9
  58.8 10.1 %reshape.208 = f32[4,4,8,4,32,4]{5,4,3,2,1,0:T(8,128)} reshape(f32[16,32,128]{2,1,0:T(8,128)S(1)} %get-tuple-element.19) | data formatting | bytes 524288 | tf_op jit(solution)/shard_map/reshape | solution.py:100
  68.9 5.9 %copy.1054 = f32[4,4,8,4,32,4]{4,1,5,3,2,0:T(4,128)S(1)} copy(f32[4,4,8,4,32,4]{5,4,3,2,1,0:T(8,128)} %reshape.208) | data formatting | bytes 524288 | tf_op jit(solution)/shard_map/reshape | solution.py:100
  82.5 4.1 all-to-all-start
  92.7 7.2 %all-to-all-start.1 = ((bf16[8,2,512]{2,1,0:T(2,128)(2,1)}), bf16[8,2,512]{2,1,0:T(2,128)(2,1)S(1)}, u32[]{:S(2)}, u32[]{:S(2)}) async-start(bf16[8,2,512]{2,1,0:T(2,128)(2,1)} %reshape.232), calls=%async_computation.1 | async-start | bytes 32768 | tf_op jit(solution)/shard_map/all_to_all | solution.py:143
  101.3 4.1 all-to-all-done.1
  106.9 9.5 %all-to-all-start.2 = ((bf16[2,128,32]{2,0,1:T(2,128)(2,1)}), bf16[2,128,32]{2,0,1:T(2,128)(2,1)S(1)}, u32[]{:S(2)}, u32[]{:S(2)}) async-start(bf16[2,128,32]{2,0,1:T(2,128)(2,1)} %copy.1062), calls=%async_computation.2 | async-start | bytes 131072 | tf_op jit(solution)/shard_map/all_to_all | solution.py:149
  117.0 5.2 %collective-permute-start.13 = (f32[1,32,128]{2,1,0:T(8,128)}, f32[1,32,128]{2,1,0:T(8,128)S(1)}, u32[]{:S(2)}, u32[]{:S(2)}) collective-permute-start(f32[1,32,128]{2,1,0:T(8,128)} %get-tuple-element.51), channel_id=1, source_target_pairs={{32,0},{64,32},{96,64},{128,96},{160,128},{192,160},{224,192},{256... | collective-permute-start | bytes 49160 | tf_op jit(solution)/shard_map/ppermute | solution.py:20
  177.5 9.4 %all-to-all-start.3 = ((bf16[64,2,2,32]{3,2,1,0:T(2,128)(2,1)}), bf16[64,2,2,32]{3,2,1,0:T(2,128)(2,1)S(1)}, u32[]{:S(2)}, u32[]{:S(2)}) async-start(bf16[64,2,2,32]{3,2,1,0:T(2,128)(2,1)} %constant_dynamic-update-slice_fusion.3), calls=%async_computation.3 | async-start | bytes 131072 | tf_op jit(solution)/shard_map/all_to_all | solution.py:173
  197.7 4.4 all-to-all-start.4
  202.2 5.6 %all-to-all-done.4 = bf16[8,2,512]{2,1,0:T(2,128)(2,1)S(1)} async-done(((bf16[8,2,512]{2,1,0:T(2,128)(2,1)}), bf16[8,2,512]{2,1,0:T(2,128)(2,1)S(1)}, u32[]{:S(2)}, u32[]{:S(2)}) %all-to-all-start.4) | async-done | bytes 16416 | tf_op jit(solution)/shard_map/all_to_all | solution.py:181
  210.8 4.6 all-to-all-start.5
  225.9 15.5 %fusion.9 = f32[4,4,8,4,32,4]{5,4,3,2,1,0:T(8,128)} fusion(f32[4,2,1,1,1,1]{0,1,5,4,3,2:T(2,128)S(1)} %copy-done.13, f32[4,4,8,4,32,2]{4,3,5,2,1,0:T(4,128)S(1)} %convolution_bitcast_fusion.2), kind=kOutput, calls=%fused_computation.37 | convolution fusion | flops 1572864 | bytes 393248 | tf_op jit(solution)/shard_map/kc,pizjyc->pizjyk/dot_general | solution.py:114
  241.4 8.2 %reshape.212 = f32[16,32,128]{2,1,0:T(8,128)S(1)} reshape(f32[4,4,8,4,32,4]{5,4,3,2,1,0:T(8,128)} %fusion.9) | data formatting | bytes 524288 | tf_op jit(solution)/shard_map/reshape | solution.py:115
  257.5 4.6 collective-permute-done.18
  269.8 4.3 collective-permute-start.23
  284.2 10.1 %reshape.213 = f32[4,4,8,4,32,4]{5,4,3,2,1,0:T(8,128)} reshape(f32[16,32,128]{2,1,0:T(8,128)S(1)} %get-tuple-element.16) | data formatting | bytes 524288 | tf_op jit(solution)/shard_map/reshape | solution.py:100
  294.3 5.9 %copy.1144 = f32[4,4,8,4,32,4]{4,1,5,3,2,0:T(4,128)S(1)} copy(f32[4,4,8,4,32,4]{5,4,3,2,1,0:T(8,128)} %reshape.213) | data formatting | bytes 524288 | tf_op jit(solution)/shard_map/reshape | solution.py:100
  308.1 7.1 %all_to_all.184 = bf16[4,2,1024]{2,1,0:T(2,128)(2,1)S(1)} all-to-all(bf16[4,2,1024]{2,1,0:T(2,128)(2,1)S(1)} %reshape.238), channel_id=1, replica_groups=mesh['bx'=16,'by'=4,'bz'=8] {'by'}, dimensions={0} | all-to-all | bytes 32768 | tf_op jit(solution)/shard_map/all_to_all | solution.py:139
  317.5 10.5 %all_to_all.185 = bf16[8,2,512]{2,1,0:T(2,128)(2,1)S(1)} all-to-all(bf16[8,2,512]{2,1,0:T(2,128)(2,1)S(1)} %reshape.240), channel_id=1, replica_groups=mesh['bx'=16,'by'=4,'bz'=8] {'bz'}, dimensions={0} | all-to-all | bytes 32768 | tf_op jit(solution)/shard_map/all_to_all | solution.py:143
  330.2 7.7 %all-to-all-start.8 = ((bf16[2,128,32]{2,0,1:T(2,128)(2,1)}), bf16[2,128,32]{2,0,1:T(2,128)(2,1)S(1)}, u32[]{:S(2)}, u32[]{:S(2)}) async-start(bf16[2,128,32]{2,0,1:T(2,128)(2,1)} %copy.1152), calls=%async_computation.8 | async-start | bytes 131072 | tf_op jit(solution)/shard_map/all_to_all | solution.py:149
  338.5 5.2 %collective-permute-start.25 = (f32[1,32,128]{2,1,0:T(8,128)}, f32[1,32,128]{2,1,0:T(8,128)S(1)}, u32[]{:S(2)}, u32[]{:S(2)}) collective-permute-start(f32[1,32,128]{2,1,0:T(8,128)} %get-tuple-element.47), channel_id=1, source_target_pairs={{32,0},{64,32},{96,64},{128,96},{160,128},{192,160},{224,192},{256... | collective-permute-start | bytes 49160 | tf_op jit(solution)/shard_map/ppermute | solution.py:20
  402.5 9.2 %all-to-all-start.9 = ((bf16[64,2,2,32]{3,2,1,0:T(2,128)(2,1)}), bf16[64,2,2,32]{3,2,1,0:T(2,128)(2,1)S(1)}, u32[]{:S(2)}, u32[]{:S(2)}) async-start(bf16[64,2,2,32]{3,2,1,0:T(2,128)(2,1)} %constant_dynamic-update-slice_fusion.67), calls=%async_computation.9 | async-start | bytes 131072 | tf_op jit(solution)/shard_map/all_to_all | solution.py:173
  422.6 4.4 all-to-all-start.10
  427.6 5.0 all-to-all-done.10
  435.6 4.6 all-to-all-start.11
  451.8 16.3 %fusion.6 = f32[4,4,8,4,32,4]{5,4,3,2,1,0:T(8,128)} fusion(f32[4,2,1,1,1,1]{0,1,5,4,3,2:T(2,128)} %constant.103, f32[4,4,8,4,32,2]{4,3,5,2,1,0:T(4,128)S(1)} %convolution_bitcast_fusion), kind=kOutput, calls=%fused_computation.34 | convolution fusion | flops 1572864 | bytes 393248 | tf_op jit(solution)/shard_map/kc,pizjyc->pizjyk/dot_general | solution.py:114
  468.1 8.8 %reshape.217 = f32[16,32,128]{2,1,0:T(8,128)} reshape(f32[4,4,8,4,32,4]{5,4,3,2,1,0:T(8,128)} %fusion.6) | data formatting | bytes 524288 | tf_op jit(solution)/shard_map/reshape | solution.py:115
  485.5 4.6 collective-permute-done.30
  497.9 4.3 collective-permute-start.35
  (524 shorter events, 280.1 us)
Async XLA Ops:
  3.3 25.4 %collective-permute-start.1 = (f32[1,32,128]{2,1,0:T(8,128)S(1)}, f32[1,32,128]{2,1,0:T(8,128)S(1)}, u32[]{:S(2)}, u32[]{:S(2)}) collective-permute-start(f32[1,32,128]{2,1,0:T(8,128)S(1)} %copy.1046), channel_id=1, source_target_pairs={{32,0},{64,32},{96,64},{128,96},{160,128},{192,160},{224,192},{256... | collective-permute-start | bytes 49160 | tf_op jit(solution)/shard_map/ppermute | solution.py:20
  14.1 14.6 %collective-permute-start = (f32[1,32,128]{2,1,0:T(8,128)S(1)}, f32[1,32,128]{2,1,0:T(8,128)S(1)}, u32[]{:S(2)}, u32[]{:S(2)}) collective-permute-start(f32[1,32,128]{2,1,0:T(8,128)S(1)} %copy.1042), channel_id=1, source_target_pairs={{0,32},{32,64},{64,96},{96,128},{128,160},{160,192},{192,224},{224... | collective-permute-start | bytes 49160 | tf_op jit(solution)/shard_map/ppermute | solution.py:19
  16.8 17.3 %collective-permute-start.2 = (f32[1,32,128]{2,1,0:T(8,128)S(1)}, f32[1,32,128]{2,1,0:T(8,128)S(1)}, u32[]{:S(2)}, u32[]{:S(2)}) collective-permute-start(f32[1,32,128]{2,1,0:T(8,128)S(1)} %get-tuple-element.53), channel_id=1, source_target_pairs={{0,32},{32,64},{64,96},{96,128},{128,160},{160,192},{192,224},{224... | collective-permute-start | bytes 49160 | tf_op jit(solution)/shard_map/ppermute | solution.py:19
  19.0 15.1 %collective-permute-start.3 = (f32[1,32,128]{2,1,0:T(8,128)S(1)}, f32[1,32,128]{2,1,0:T(8,128)S(1)}, u32[]{:S(2)}, u32[]{:S(2)}) collective-permute-start(f32[1,32,128]{2,1,0:T(8,128)S(1)} %get-tuple-element.52), channel_id=1, source_target_pairs={{32,0},{64,32},{96,64},{128,96},{160,128},{192,160},{224,192},{256... | collective-permute-start | bytes 49160 | tf_op jit(solution)/shard_map/ppermute | solution.py:20
  28.7 10.8 %collective-permute-start.5 = (f32[18,1,128]{2,1,0:T(1,128)S(1)}, f32[18,1,128]{2,1,0:T(1,128)S(1)}, u32[]{:S(2)}, u32[]{:S(2)}) collective-permute-start(f32[18,1,128]{2,1,0:T(1,128)S(1)} %get-tuple-element.43), channel_id=1, source_target_pairs={{1,0},{2,1},{3,2},{4,3},{5,4},{6,5},{7,6},{9,8},{10,9},{11,10},{12... | collective-permute-start | bytes 27656 | tf_op jit(solution)/shard_map/ppermute | solution.py:20
  34.1 13.2 %collective-permute-start.7 = (f32[18,1,128]{2,1,0:T(1,128)S(1)}, f32[18,1,128]{2,1,0:T(1,128)S(1)}, u32[]{:S(2)}, u32[]{:S(2)}) collective-permute-start(f32[18,1,128]{2,1,0:T(1,128)S(1)} %get-tuple-element.41), channel_id=1, source_target_pairs={{1,0},{2,1},{3,2},{4,3},{5,4},{6,5},{7,6},{9,8},{10,9},{11,10},{12... | collective-permute-start | bytes 27656 | tf_op jit(solution)/shard_map/ppermute | solution.py:20
  36.2 11.1 %collective-permute-start.6 = (f32[18,1,128]{2,1,0:T(1,128)S(1)}, f32[18,1,128]{2,1,0:T(1,128)S(1)}, u32[]{:S(2)}, u32[]{:S(2)}) collective-permute-start(f32[18,1,128]{2,1,0:T(1,128)S(1)} %get-tuple-element.40), channel_id=1, source_target_pairs={{0,1},{1,2},{2,3},{3,4},{4,5},{5,6},{6,7},{8,9},{9,10},{10,11},{11... | collective-permute-start | bytes 27656 | tf_op jit(solution)/shard_map/ppermute | solution.py:19
  39.8 13.7 %collective-permute-start.9 = (f32[18,34,1]{2,1,0:T(8,128)S(1)}, f32[18,34,1]{2,1,0:T(8,128)S(1)}, u32[]{:S(2)}, u32[]{:S(2)}) collective-permute-start(f32[18,34,1]{2,1,0:T(8,128)S(1)} %get-tuple-element.31), channel_id=1, source_target_pairs={{8,0},{16,8},{24,16},{9,1},{17,9},{25,17},{10,2},{18,10},{26,18},{... | collective-permute-start | bytes 7352 | tf_op jit(solution)/shard_map/ppermute | solution.py:20
  44.3 9.1 %collective-permute-start.8 = (f32[18,34,1]{2,1,0:T(8,128)S(1)}, f32[18,34,1]{2,1,0:T(8,128)S(1)}, u32[]{:S(2)}, u32[]{:S(2)}) collective-permute-start(f32[18,34,1]{2,1,0:T(8,128)S(1)} %get-tuple-element.30), channel_id=1, source_target_pairs={{0,8},{8,16},{16,24},{1,9},{9,17},{17,25},{2,10},{10,18},{18,26},{... | collective-permute-start | bytes 7352 | tf_op jit(solution)/shard_map/ppermute | solution.py:19
  92.7 12.7 %all-to-all-start.1 = ((bf16[8,2,512]{2,1,0:T(2,128)(2,1)}), bf16[8,2,512]{2,1,0:T(2,128)(2,1)S(1)}, u32[]{:S(2)}, u32[]{:S(2)}) async-start(bf16[8,2,512]{2,1,0:T(2,128)(2,1)} %reshape.232), calls=%async_computation.1 | async-start | bytes 32768 | tf_op jit(solution)/shard_map/all_to_all | solution.py:143
  106.9 18.4 %all-to-all-start.2 = ((bf16[2,128,32]{2,0,1:T(2,128)(2,1)}), bf16[2,128,32]{2,0,1:T(2,128)(2,1)S(1)}, u32[]{:S(2)}, u32[]{:S(2)}) async-start(bf16[2,128,32]{2,0,1:T(2,128)(2,1)} %copy.1062), calls=%async_computation.2 | async-start | bytes 131072 | tf_op jit(solution)/shard_map/all_to_all | solution.py:149
  117.0 69.9 %collective-permute-start.13 = (f32[1,32,128]{2,1,0:T(8,128)}, f32[1,32,128]{2,1,0:T(8,128)S(1)}, u32[]{:S(2)}, u32[]{:S(2)}) collective-permute-start(f32[1,32,128]{2,1,0:T(8,128)} %get-tuple-element.51), channel_id=1, source_target_pairs={{32,0},{64,32},{96,64},{128,96},{160,128},{192,160},{224,192},{256... | collective-permute-start | bytes 49160 | tf_op jit(solution)/shard_map/ppermute | solution.py:20
  122.2 64.7 %collective-permute-start.12 = (f32[1,32,128]{2,1,0:T(8,128)}, f32[1,32,128]{2,1,0:T(8,128)S(1)}, u32[]{:S(2)}, u32[]{:S(2)}) collective-permute-start(f32[1,32,128]{2,1,0:T(8,128)} %get-tuple-element.50), channel_id=1, source_target_pairs={{0,32},{32,64},{64,96},{96,128},{128,160},{160,192},{192,224},{224... | collective-permute-start | bytes 49160 | tf_op jit(solution)/shard_map/ppermute | solution.py:19
  177.5 18.3 %all-to-all-start.3 = ((bf16[64,2,2,32]{3,2,1,0:T(2,128)(2,1)}), bf16[64,2,2,32]{3,2,1,0:T(2,128)(2,1)S(1)}, u32[]{:S(2)}, u32[]{:S(2)}) async-start(bf16[64,2,2,32]{3,2,1,0:T(2,128)(2,1)} %constant_dynamic-update-slice_fusion.3), calls=%async_computation.3 | async-start | bytes 131072 | tf_op jit(solution)/shard_map/all_to_all | solution.py:173
  187.0 15.2 %collective-permute-start.15 = (f32[18,1,128]{2,1,0:T(1,128)S(1)}, f32[18,1,128]{2,1,0:T(1,128)S(1)}, u32[]{:S(2)}, u32[]{:S(2)}) collective-permute-start(f32[18,1,128]{2,1,0:T(1,128)S(1)} %get-tuple-element.39), channel_id=1, source_target_pairs={{1,0},{2,1},{3,2},{4,3},{5,4},{6,5},{7,6},{9,8},{10,9},{11,10},{12... | collective-permute-start | bytes 27656 | tf_op jit(solution)/shard_map/ppermute | solution.py:20
  190.0 12.1 %collective-permute-start.14 = (f32[18,1,128]{2,1,0:T(1,128)S(1)}, f32[18,1,128]{2,1,0:T(1,128)S(1)}, u32[]{:S(2)}, u32[]{:S(2)}) collective-permute-start(f32[18,1,128]{2,1,0:T(1,128)S(1)} %get-tuple-element.38), channel_id=1, source_target_pairs={{0,1},{1,2},{2,3},{3,4},{4,5},{5,6},{6,7},{8,9},{9,10},{10,11},{11... | collective-permute-start | bytes 27656 | tf_op jit(solution)/shard_map/ppermute | solution.py:19
  197.7 10.0 %all-to-all-start.4 = ((bf16[8,2,512]{2,1,0:T(2,128)(2,1)}), bf16[8,2,512]{2,1,0:T(2,128)(2,1)S(1)}, u32[]{:S(2)}, u32[]{:S(2)}) async-start(bf16[8,2,512]{2,1,0:T(2,128)(2,1)} %reshape.234), calls=%async_computation.4 | async-start | bytes 32768 | tf_op jit(solution)/shard_map/all_to_all | solution.py:181
  210.8 11.6 %all-to-all-start.5 = ((bf16[4,2,1024]{2,1,0:T(2,128)(2,1)}), bf16[4,2,1024]{2,1,0:T(2,128)(2,1)S(1)}, u32[]{:S(2)}, u32[]{:S(2)}) async-start(bf16[4,2,1024]{2,1,0:T(2,128)(2,1)} %reshape.236), calls=%async_computation.5 | async-start | bytes 32768 | tf_op jit(solution)/shard_map/all_to_all | solution.py:183
  216.4 33.2 %collective-permute-start.17 = (f32[18,34,1]{2,1,0:T(8,128)}, f32[18,34,1]{2,1,0:T(8,128)}, u32[]{:S(2)}, u32[]{:S(2)}) collective-permute-start(f32[18,34,1]{2,1,0:T(8,128)} %get-tuple-element.27), channel_id=1, source_target_pairs={{8,0},{16,8},{24,16},{9,1},{17,9},{25,17},{10,2},{18,10},{26,18},{... | collective-permute-start | bytes 7352 | tf_op jit(solution)/shard_map/ppermute | solution.py:20
  218.3 31.3 %collective-permute-start.16 = (f32[18,34,1]{2,1,0:T(8,128)}, f32[18,34,1]{2,1,0:T(8,128)}, u32[]{:S(2)}, u32[]{:S(2)}) collective-permute-start(f32[18,34,1]{2,1,0:T(8,128)} %get-tuple-element.26), channel_id=1, source_target_pairs={{0,8},{8,16},{16,24},{1,9},{9,17},{17,25},{2,10},{10,18},{18,26},{... | collective-permute-start | bytes 7352 | tf_op jit(solution)/shard_map/ppermute | solution.py:19
  269.8 11.1 %collective-permute-start.23 = (f32[18,34,1]{2,1,0:T(8,128)S(1)}, f32[18,34,1]{2,1,0:T(8,128)S(1)}, u32[]{:S(2)}, u32[]{:S(2)}) collective-permute-start(f32[18,34,1]{2,1,0:T(8,128)S(1)} %get-tuple-element.25), channel_id=1, source_target_pairs={{8,0},{16,8},{24,16},{9,1},{17,9},{25,17},{10,2},{18,10},{26,18},{... | collective-permute-start | bytes 7352 | tf_op jit(solution)/shard_map/ppermute | solution.py:20
  330.2 16.5 %all-to-all-start.8 = ((bf16[2,128,32]{2,0,1:T(2,128)(2,1)}), bf16[2,128,32]{2,0,1:T(2,128)(2,1)S(1)}, u32[]{:S(2)}, u32[]{:S(2)}) async-start(bf16[2,128,32]{2,0,1:T(2,128)(2,1)} %copy.1152), calls=%async_computation.8 | async-start | bytes 131072 | tf_op jit(solution)/shard_map/all_to_all | solution.py:149
  338.5 73.2 %collective-permute-start.25 = (f32[1,32,128]{2,1,0:T(8,128)}, f32[1,32,128]{2,1,0:T(8,128)S(1)}, u32[]{:S(2)}, u32[]{:S(2)}) collective-permute-start(f32[1,32,128]{2,1,0:T(8,128)} %get-tuple-element.47), channel_id=1, source_target_pairs={{32,0},{64,32},{96,64},{128,96},{160,128},{192,160},{224,192},{256... | collective-permute-start | bytes 49160 | tf_op jit(solution)/shard_map/ppermute | solution.py:20
  343.7 68.0 %collective-permute-start.24 = (f32[1,32,128]{2,1,0:T(8,128)}, f32[1,32,128]{2,1,0:T(8,128)S(1)}, u32[]{:S(2)}, u32[]{:S(2)}) collective-permute-start(f32[1,32,128]{2,1,0:T(8,128)} %get-tuple-element.46), channel_id=1, source_target_pairs={{0,32},{32,64},{64,96},{96,128},{128,160},{160,192},{192,224},{224... | collective-permute-start | bytes 49160 | tf_op jit(solution)/shard_map/ppermute | solution.py:19
  402.5 18.0 %all-to-all-start.9 = ((bf16[64,2,2,32]{3,2,1,0:T(2,128)(2,1)}), bf16[64,2,2,32]{3,2,1,0:T(2,128)(2,1)S(1)}, u32[]{:S(2)}, u32[]{:S(2)}) async-start(bf16[64,2,2,32]{3,2,1,0:T(2,128)(2,1)} %constant_dynamic-update-slice_fusion.67), calls=%async_computation.9 | async-start | bytes 131072 | tf_op jit(solution)/shard_map/all_to_all | solution.py:173
  411.8 15.2 %collective-permute-start.27 = (f32[18,1,128]{2,1,0:T(1,128)S(1)}, f32[18,1,128]{2,1,0:T(1,128)S(1)}, u32[]{:S(2)}, u32[]{:S(2)}) collective-permute-start(f32[18,1,128]{2,1,0:T(1,128)S(1)} %get-tuple-element.35), channel_id=1, source_target_pairs={{1,0},{2,1},{3,2},{4,3},{5,4},{6,5},{7,6},{9,8},{10,9},{11,10},{12... | collective-permute-start | bytes 27656 | tf_op jit(solution)/shard_map/ppermute | solution.py:20
  414.8 12.1 %collective-permute-start.26 = (f32[18,1,128]{2,1,0:T(1,128)S(1)}, f32[18,1,128]{2,1,0:T(1,128)S(1)}, u32[]{:S(2)}, u32[]{:S(2)}) collective-permute-start(f32[18,1,128]{2,1,0:T(1,128)S(1)} %get-tuple-element.34), channel_id=1, source_target_pairs={{0,1},{1,2},{2,3},{3,4},{4,5},{5,6},{6,7},{8,9},{9,10},{10,11},{11... | collective-permute-start | bytes 27656 | tf_op jit(solution)/shard_map/ppermute | solution.py:19
  422.6 10.0 %all-to-all-start.10 = ((bf16[8,2,512]{2,1,0:T(2,128)(2,1)}), bf16[8,2,512]{2,1,0:T(2,128)(2,1)S(1)}, u32[]{:S(2)}, u32[]{:S(2)}) async-start(bf16[8,2,512]{2,1,0:T(2,128)(2,1)} %reshape.242), calls=%async_computation.10 | async-start | bytes 32768 | tf_op jit(solution)/shard_map/all_to_all | solution.py:181
  435.6 11.4 %all-to-all-start.11 = ((bf16[4,2,1024]{2,1,0:T(2,128)(2,1)}), bf16[4,2,1024]{2,1,0:T(2,128)(2,1)S(1)}, u32[]{:S(2)}, u32[]{:S(2)}) async-start(bf16[4,2,1024]{2,1,0:T(2,128)(2,1)} %reshape.244), calls=%async_computation.11 | async-start | bytes 32768 | tf_op jit(solution)/shard_map/all_to_all | solution.py:183
  441.2 35.7 %collective-permute-start.29 = (f32[18,34,1]{2,1,0:T(8,128)}, f32[18,34,1]{2,1,0:T(8,128)}, u32[]{:S(2)}, u32[]{:S(2)}) collective-permute-start(f32[18,34,1]{2,1,0:T(8,128)} %get-tuple-element.23), channel_id=1, source_target_pairs={{8,0},{16,8},{24,16},{9,1},{17,9},{25,17},{10,2},{18,10},{26,18},{... | collective-permute-start | bytes 7352 | tf_op jit(solution)/shard_map/ppermute | solution.py:20
  443.1 33.8 %collective-permute-start.28 = (f32[18,34,1]{2,1,0:T(8,128)}, f32[18,34,1]{2,1,0:T(8,128)}, u32[]{:S(2)}, u32[]{:S(2)}) collective-permute-start(f32[18,34,1]{2,1,0:T(8,128)} %get-tuple-element.22), channel_id=1, source_target_pairs={{0,8},{8,16},{16,24},{1,9},{9,17},{17,25},{2,10},{10,18},{18,26},{... | collective-permute-start | bytes 7352 | tf_op jit(solution)/shard_map/ppermute | solution.py:19
  497.9 11.1 %collective-permute-start.35 = (f32[18,34,1]{2,1,0:T(8,128)S(1)}, f32[18,34,1]{2,1,0:T(8,128)S(1)}, u32[]{:S(2)}, u32[]{:S(2)}) collective-permute-start(f32[18,34,1]{2,1,0:T(8,128)S(1)} %get-tuple-element.21), channel_id=1, source_target_pairs={{8,0},{16,8},{24,16},{9,1},{17,9},{25,17},{10,2},{18,10},{26,18},{... | collective-permute-start | bytes 7352 | tf_op jit(solution)/shard_map/ppermute | solution.py:20
  (34 other events, 900.8 us)
